TPU v7x, 32 devices: a whole 2x2x4 slice. The times are simulated.
32 devices in a mesh: tm: 2 (over x), seq: 16 (over z, y, core).
Axes of the slice: x: 2, y: 2, z: 4, core: 2. Of those that a mesh axis runs over, the one named last changes fastest.
Arguments:
- tokens: bfloat16 [512, 5120], P(('tm', 'seq')), may hold values from -6 to 6
- w_query: bfloat16 [5120, 4096], P('seq'), may hold values from -0.078125 to 0.078125
- w_out: bfloat16 [4096, 5120], P(None, 'seq'), may hold values from -0.25 to 0.25
- k_cache: bfloat16 [4096, 4096], P(('tm', 'seq')), may hold values from -800 to 800
- v_cache: bfloat16 [4096, 4096], P(('tm', 'seq')), may hold values from -6 to 6
- radial_mask: int32 [16, 2, 32], replicated, may hold values from 0 to 1, as said below
- slot_frame: int32 [16], replicated, may hold values from 0 to 15, each once
Outputs:
- mixed: bfloat16 [512, 5120], P(('tm', 'seq'))
Inputs may be any that keep to these rules, and one draw needn't show every extreme that they name: radial_mask[f, b, f * 2 + b] = 1 for every frame f and tile b. `slot_frame`: each of the 16 frames is held by exactly one slot.
All inputs are finite; a program needn't handle non-finite values.
Results may differ from a plain program's by a relative error of at most 0.012.
The roundings to bfloat16 on the way count: a program that leaves them out, or rounds other values in their place, can miss the bound.
Values may be sent and summed in bfloat16 or wider, within the bound.
A program may use at most 128 MiB of HBM per device.

v0:
```python
import jax
import jax.numpy as jnp
from jax import lax
from jax.sharding import PartitionSpec as P

D = 5120
HD = 128
HEADS = 32
FRAMES = 16
BLOCK = 128
Q_DEV = 16
NEG = -1e30


def spread_columns(table, blocks, copies, groups):
    rows = table.shape[0]
    head_width = table.shape[1] // blocks
    grouped = table.reshape(rows, 1, blocks, 1, head_width)
    spread = jnp.broadcast_to(grouped, (rows, groups, blocks, copies, head_width))
    return spread.reshape(rows, groups * blocks * copies, head_width)


def on_device(tokens, w_query, w_out, k_cache, v_cache, radial_mask, slot_frame):
    seq_count = lax.axis_size("seq")
    group_count = lax.axis_size("tm")
    copies = max(1, seq_count // HEADS)
    per_dev = HEADS * copies // seq_count
    head_width = per_dev * HD
    blocks = seq_count // copies
    part_rows = Q_DEV // copies
    query_rows = part_rows * seq_count
    frame_tok = Q_DEV * seq_count
    frame_blocks = frame_tok // BLOCK
    per_group = FRAMES // group_count
    key_tile = 4 * BLOCK
    score_scale = HD ** (-0.5)
    my_seq = lax.axis_index("seq")
    my_group = lax.axis_index("tm")
    my_part = my_seq % copies
    split_rows = (
        tokens.reshape(copies, part_rows, D).transpose(1, 0, 2).reshape(part_rows, 1, copies, D)
    )
    token_send = jnp.broadcast_to(split_rows, (part_rows, blocks, copies, D)).reshape(
        part_rows, seq_count, D
    )
    query_send = spread_columns(w_query, blocks, copies, 1)
    frame = lax.dynamic_index_in_dim(slot_frame, my_group * per_group, 0, keepdims=False)
    onehot = (slot_frame[:, None] == lax.iota(jnp.int32, FRAMES)[None, :]).astype(jnp.float32)
    chosen = lax.dynamic_index_in_dim(radial_mask, frame, 0, keepdims=False).astype(jnp.float32)
    chosen = chosen.reshape(frame_blocks, FRAMES, frame_blocks)
    mask_slots = jnp.einsum("sf,qfb->qsb", onehot, chosen).reshape(
        frame_blocks, FRAMES * frame_blocks
    )
    row_index = lax.iota(jnp.int32, query_rows)
    token_index = row_index // part_rows * Q_DEV + my_part * part_rows + row_index % part_rows
    row_block = (token_index // BLOCK)[:, None] == lax.iota(jnp.int32, frame_blocks)[None, :]
    row_allowed = jnp.dot(
        row_block.astype(jnp.float32), mask_slots, preferred_element_type=jnp.float32
    )
    key_send = spread_columns(k_cache, blocks, copies, 1)
    value_send = spread_columns(v_cache, blocks, copies, 1)
    token_got, query_got, key_got, value_got = (
        lax.all_to_all(token_send, "seq", split_axis=1, concat_axis=0, tiled=True),
        lax.all_to_all(query_send, "seq", split_axis=1, concat_axis=0, tiled=True),
        lax.all_to_all(key_send, "seq", split_axis=1, concat_axis=0, tiled=True),
        lax.all_to_all(value_send, "seq", split_axis=1, concat_axis=0, tiled=True),
    )
    query = jnp.dot(
        token_got.reshape(query_rows, D),
        query_got.reshape(D, head_width),
        preferred_element_type=jnp.float32,
    )
    query = query.astype(jnp.bfloat16).reshape(query_rows, per_dev, HD)
    start_state = (
        jnp.full((query_rows, per_dev), NEG, jnp.float32),
        jnp.zeros((query_rows, per_dev), jnp.float32),
        jnp.zeros((query_rows, per_dev, HD), jnp.float32),
    )
    group_keys = key_got.reshape(-1, head_width)
    group_values = value_got.reshape(-1, head_width)
    keys = lax.all_gather(group_keys, "tm", axis=0, tiled=True)
    values = lax.all_gather(group_values, "tm", axis=0, tiled=True)
    tiles = keys.shape[0] // key_tile

    def one_tile(index, state):
        highest, denom, summed = state
        k_tile = lax.dynamic_slice_in_dim(keys, index * key_tile, key_tile, 0).reshape(
            key_tile, per_dev, HD
        )
        v_tile = lax.dynamic_slice_in_dim(values, index * key_tile, key_tile, 0).reshape(
            key_tile, per_dev, HD
        )
        first_block = index * key_tile // BLOCK
        allowed = lax.dynamic_slice_in_dim(row_allowed, first_block, key_tile // BLOCK, 1)
        keep = jnp.repeat(allowed > 0.5, BLOCK, axis=1)[:, None, :]
        scores = (
            jnp.einsum("qhd,khd->qhk", query, k_tile, preferred_element_type=jnp.float32)
            * score_scale
        )
        scores = jnp.where(keep, scores, NEG)
        new_high = jnp.maximum(highest, jnp.max(scores, axis=2))
        weights = jnp.where(keep, jnp.exp(scores - new_high[..., None]), 0.0)
        fade = jnp.exp(highest - new_high)
        denom = denom * fade + jnp.sum(weights, axis=2)
        update = jnp.einsum(
            "qhk,khd->qhd", weights.astype(jnp.bfloat16), v_tile, preferred_element_type=jnp.float32
        )
        summed = summed * fade[..., None] + update
        return (new_high, denom, summed)

    final_state = lax.fori_loop(0, tiles, one_tile, start_state)
    attended = (
        (final_state[2] / final_state[1][..., None])
        .astype(jnp.bfloat16)
        .reshape(query_rows, head_width)
    )
    out_columns = w_out.shape[1]
    every_head = lax.all_gather(attended[None], "seq", axis=0, tiled=True)
    every_head = every_head.reshape(blocks, copies, seq_count, part_rows, head_width)
    w_blocks = w_out.reshape(blocks, head_width, out_columns)
    columns = jnp.einsum(
        "bcsrw,bwo->scro", every_head, w_blocks, preferred_element_type=jnp.float32
    )
    columns = columns.reshape(frame_tok, out_columns).astype(jnp.bfloat16)
    mixed = lax.all_to_all(columns, "seq", split_axis=0, concat_axis=1, tiled=True)
    return mixed


def solution(mesh):
    return jax.shard_map(
        on_device,
        mesh=mesh,
        in_specs=(
            P(("tm", "seq"), None),
            P("seq", None),
            P(None, "seq"),
            P(("tm", "seq"), None),
            P(("tm", "seq"), None),
            P(),
            P(),
        ),
        out_specs=P(("tm", "seq"), None),
        check_vma=False,
    )
```

profile of v0, /device:TPU:0, one launch (start us, length us, event | category | flops | bytes accessed | tf_op | source)
XLA Modules:
  0.0 300.3 jit_solution(17684607203295914071)
XLA Ops:
  6.5 2.4 copy.52
  8.9 7.4 %all-to-all-start = ((bf16[128,16,256]{0,2,1:T(8,128)(2,1)}), bf16[128,16,256]{0,2,1:T(8,128)(2,1)S(1)}, u32[]{:S(2)}, u32[]{:S(2)}) async-start(bf16[128,16,256]{0,2,1:T(8,128)(2,1)} %bitcast.3), calls=%async_computation | async-start | bytes 2097152 | tf_op jit(solution)/shard_map/all_to_all | solution.py:65
  16.3 1.3 copy.55
  17.6 21.6 %all-to-all-done = bf16[128,16,256]{0,2,1:T(8,128)(2,1)S(1)} async-done(((bf16[128,16,256]{0,2,1:T(8,128)(2,1)}), bf16[128,16,256]{0,2,1:T(8,128)(2,1)S(1)}, u32[]{:S(2)}, u32[]{:S(2)}) %all-to-all-start) | async-done | bytes 1048608 | tf_op jit(solution)/shard_map/all_to_all | solution.py:65
  39.2 1.0 copy-done.1
  40.2 6.8 %all-to-all-start.3 = ((bf16[128,16,256]{0,2,1:T(8,128)(2,1)}), bf16[128,16,256]{0,2,1:T(8,128)(2,1)S(1)}, u32[]{:S(2)}, u32[]{:S(2)}) async-start(bf16[128,16,256]{0,2,1:T(8,128)(2,1)} %bitcast.14), calls=%async_computation.3 | async-start | bytes 2097152 | tf_op jit(solution)/shard_map/all_to_all | solution.py:66
  47.0 3.5 %copy.81 = bf16[40,16,8,256]{3,2,0,1:T(8,128)(2,1)} copy(bf16[40,16,8,256]{3,2,1,0:T(8,128)(2,1)} %bitcast.88) | data formatting | bytes 5242880 | tf_op jit(solution)/shard_map/reshape;reshape | solution.py:20
  50.5 19.4 %all-to-all-done.3 = bf16[128,16,256]{0,2,1:T(8,128)(2,1)S(1)} async-done(((bf16[128,16,256]{0,2,1:T(8,128)(2,1)}), bf16[128,16,256]{0,2,1:T(8,128)(2,1)S(1)}, u32[]{:S(2)}, u32[]{:S(2)}) %all-to-all-start.3) | async-done | bytes 1048608 | tf_op jit(solution)/shard_map/all_to_all | solution.py:66
  69.9 1.0 copy-done
  70.9 65.3 %all_to_all.76 = bf16[320,16,256]{2,0,1:T(8,128)(2,1)S(1)} all-to-all(bf16[320,16,256]{2,0,1:T(8,128)(2,1)} %bitcast.85), channel_id=1, replica_groups=mesh['tm'=2,'seq'=16] {'seq'}, dimensions={1} | all-to-all | bytes 5242880 | tf_op jit(solution)/shard_map/all_to_all | solution.py:64
  136.2 1.8 reshape.112
  138.1 5.2 %all-to-all-start.1 = ((bf16[16,16,5120]{2,0,1:T(8,128)(2,1)}), bf16[16,16,5120]{2,0,1:T(8,128)(2,1)}, u32[]{:S(2)}, u32[]{:S(2)}) async-start(bf16[16,16,5120]{2,0,1:T(8,128)(2,1)} %reshape.112), calls=%async_computation.1 | async-start | bytes 5242880 | tf_op jit(solution)/shard_map/all_to_all | solution.py:63
  143.4 2.3 copy.53
  145.7 2.3 copy.56
  148.1 0.6 dynamic_slice.38
  150.4 0.7 dynamic-slice_convert_fusion
  151.2 0.2 convolution_bitcast_fusion.1
  151.6 0.2 fusion.20
  151.9 41.6 %all-to-all-done.1 = bf16[16,16,5120]{2,0,1:T(8,128)(2,1)} async-done(((bf16[16,16,5120]{2,0,1:T(8,128)(2,1)}), bf16[16,16,5120]{2,0,1:T(8,128)(2,1)}, u32[]{:S(2)}, u32[]{:S(2)}) %all-to-all-start.1) | async-done | bytes 2621472 | tf_op jit(solution)/shard_map/all_to_all | solution.py:63
  193.5 2.9 convolution_convert_fusion
  196.5 18.4 %all-gather.6.cloned.1.call-done = bf16[4096,256]{1,0:T(8,128)(2,1)} async-done(((bf16[2048,256]{1,0:T(8,128)(2,1)}), bf16[4096,256]{1,0:T(8,128)(2,1)}) %all-gather.6.cloned.1.call-update) | async-done | bytes 2097168 | tf_op jit(solution)/shard_map/all_gather | solution.py:82
  214.9 20.1 %while.20 = (s32[]{:T(128)}, f32[256,2]{0,1:T(2,128)S(1)}, f32[256,2]{0,1:T(2,128)S(1)}, f32[256,2,128]{0,2,1:T(8,128)S(1)}, f32[256,32]{0,1:T(8,128)S(1)}, /*in...) while((s32[]{:T(128)}, f32[256,2]{0,1:T(2,128)S(1)}, ...), condition=%wide.region_3.4_spmd.clone, body=%wide.region_0.3_spmd.clone.sunk | while | flops 136777248 | bytes 6986118 | solution.py:111
  214.9 1.1 constant_dynamic-slice_fusion.3
  216.1 0.4 fusion.51
  216.5 0.2 fusion.53
  216.8 0.1 copy.85
  216.9 0.4 fusion.55
  217.4 1.1 constant_dynamic-slice_fusion.3
  218.6 0.4 fusion.51
  219.0 0.2 fusion.53
  219.3 0.1 copy.85
  219.4 0.4 fusion.55
  219.9 1.1 constant_dynamic-slice_fusion.3
  221.2 0.4 fusion.51
  221.5 0.2 fusion.53
  221.8 0.1 copy.85
  221.9 0.4 fusion.55
  222.5 1.1 constant_dynamic-slice_fusion.3
  223.7 0.4 fusion.51
  224.1 0.2 fusion.53
  224.3 0.1 copy.85
  224.5 0.4 fusion.55
  225.0 1.1 constant_dynamic-slice_fusion.3
  226.2 0.4 fusion.51
  226.6 0.2 fusion.53
  227.0 0.4 fusion.55
  227.5 1.1 constant_dynamic-slice_fusion.3
  228.7 0.4 fusion.51
  229.1 0.2 fusion.53
  229.5 0.4 fusion.55
  230.0 1.1 constant_dynamic-slice_fusion.3
  231.2 0.4 fusion.51
  231.6 0.2 fusion.53
  232.0 0.4 fusion.55
  232.5 1.1 constant_dynamic-slice_fusion.3
  233.7 0.4 fusion.51
  234.1 0.2 fusion.53
  234.5 0.4 fusion.55
  235.0 0.8 copy.67
  235.8 2.6 copy.73
  238.3 39.0 %all-gather.8.cloned.1.call-done = bf16[16,256,256]{2,1,0:T(8,128)(2,1)} async-done(((bf16[1,256,256]{2,1,0:T(8,128)(2,1)}), bf16[16,256,256]{2,1,0:T(8,128)(2,1)}) %all-gather.8.cloned.1.call-update) | async-done | bytes 2097168 | tf_op jit(solution)/shard_map/all_gather | solution.py:118
  277.4 3.3 %fusion.17 = bf16[16,16,320]{2,1,0:T(8,128)(2,1)S(1)} fusion(bf16[16,16,16,256]{3,2,1,0:T(8,128)(2,1)} %bitcast.94, bf16[16,256,320,1]{1,0,2,3:T(8,128)(2,1)S(1)} %bitcast.90), kind=kOutput, calls=%fused_computation.25 | convolution fusion | flops 671170560 | bytes 4882432 | tf_op jit(solution)/shard_map/bcsrw,bwo->scro/dot_general | solution.py:121
  280.7 12.2 %all_to_all.77 = bf16[16,16,320]{2,1,0:T(8,128)(2,1)S(1)} all-to-all(bf16[16,16,320]{2,1,0:T(8,128)(2,1)S(1)} %fusion.17), channel_id=1, replica_groups=mesh['tm'=2,'seq'=16] {'seq'}, dimensions={0} | all-to-all | bytes 327680 | tf_op jit(solution)/shard_map/all_to_all | solution.py:125
  292.9 0.8 all_to_all.70
  (77 shorter events, 3.0 us)
Async XLA Ops:
  6.5 9.8 %copy-start.2 = (bf16[128,4096]{1,0:T(8,128)(2,1)S(1)}, bf16[128,4096]{1,0:T(8,128)(2,1)}, u32[]{:S(2)}) copy-start(bf16[128,4096]{1,0:T(8,128)(2,1)} %param.13) | copy-start | bytes 3145732
  8.9 30.3 %all-to-all-start = ((bf16[128,16,256]{0,2,1:T(8,128)(2,1)}), bf16[128,16,256]{0,2,1:T(8,128)(2,1)S(1)}, u32[]{:S(2)}, u32[]{:S(2)}) async-start(bf16[128,16,256]{0,2,1:T(8,128)(2,1)} %bitcast.3), calls=%async_computation | async-start | bytes 2097152 | tf_op jit(solution)/shard_map/all_to_all | solution.py:65
  39.2 1.0 copy-start.1
  40.2 29.7 %all-to-all-start.3 = ((bf16[128,16,256]{0,2,1:T(8,128)(2,1)}), bf16[128,16,256]{0,2,1:T(8,128)(2,1)S(1)}, u32[]{:S(2)}, u32[]{:S(2)}) async-start(bf16[128,16,256]{0,2,1:T(8,128)(2,1)} %bitcast.14), calls=%async_computation.3 | async-start | bytes 2097152 | tf_op jit(solution)/shard_map/all_to_all | solution.py:66
  69.9 1.0 copy-start
  70.9 65.3 %copy-start.3 = (bf16[16,5120]{1,0:T(8,128)(2,1)S(1)}, bf16[16,5120]{1,0:T(8,128)(2,1)}, u32[]{:S(2)}) copy-start(bf16[16,5120]{1,0:T(8,128)(2,1)} %param.9) | copy-start | bytes 491524
  138.1 55.4 %all-to-all-start.1 = ((bf16[16,16,5120]{2,0,1:T(8,128)(2,1)}), bf16[16,16,5120]{2,0,1:T(8,128)(2,1)}, u32[]{:S(2)}, u32[]{:S(2)}) async-start(bf16[16,16,5120]{2,0,1:T(8,128)(2,1)} %reshape.112), calls=%async_computation.1 | async-start | bytes 5242880 | tf_op jit(solution)/shard_map/all_to_all | solution.py:63
  143.3 53.2 %all-gather.4.cloned.1.call-start = ((), (), s32[]{:S(2)}) async-start(), calls=%async_computation.5 | async-start | bytes 3145728 | tf_op jit(solution)/shard_map/all_gather | solution.py:81
  145.6 2.4 copy-start.4
  145.7 69.2 %all-gather.6.cloned.1.call-start = ((), (), s32[]{:S(2)}) async-start(), calls=%async_computation.6 | async-start | bytes 3145728 | tf_op jit(solution)/shard_map/all_gather | solution.py:82
  148.0 129.4 %all-gather.8.cloned.1.call-start = ((), (), s32[]{:S(2)}) async-start(), calls=%async_computation.7 | async-start | bytes 2228224 | tf_op jit(solution)/shard_map/all_gather | solution.py:118
Sparse Core Ops, SparseCore 0:
  145.8 34.3 all-gather.3
  181.7 33.0 all-gather.5
  235.9 41.4 all-gather.7
where the time goes:
time: 301 us; the launch traced here: 300 us
  waiting for transfers between devices  140 us (47%)
  blocking collectives  77.5 us (26%)
  local copies, waits for them, and re-layouts  32 us (11%)
  starting transfers between devices  19.5 us (6%)
  between operations  15 us (5%)
  matrix products  12.6 us (4%)
    all_to_all x1, blocking collectives, on_device(): lax.all_to_all(query_send, 'seq', split_axis=1, concat_axis=0, tiled=True)  65.3 us
    all_to_all x1, waiting for transfers between devices, on_device(): lax.all_to_all(token_send, 'seq', split_axis=1, concat_axis=0, tiled=True)  41.6 us
    all_gather x1, waiting for transfers between devices, on_device(): every_head = lax.all_gather(attended[None], 'seq', axis=0, tiled=True)  39 us
    all_to_all x1, waiting for transfers between devices, on_device(): lax.all_to_all(key_send, 'seq', split_axis=1, concat_axis=0, tiled=True)  21.6 us
    all_to_all x1, waiting for transfers between devices, on_device(): lax.all_to_all(value_send, 'seq', split_axis=1, concat_axis=0, tiled=True)  19.4 us
    all_gather x1, waiting for transfers between devices, on_device(): values = lax.all_gather(group_values, 'tm', axis=0, tiled=True)  18.4 us
    all_to_all x1, blocking collectives, on_device(): lax.all_to_all(columns, 'seq', split_axis=0, concat_axis=1, tiled=True)  12.2 us
    dynamic_slice x16, local copies, waits for them, and re-layouts, one_tile(): lax.dynamic_slice_in_dim(values, index * key_tile, key_tile, 0)  9.69 us
  transfers between devices with their start and end apart: 6, of which 5 were waited for; matrix products, arithmetic and copies ran while one was open for 6% of the time, Pallas kernels for 0%

commit v1 on v0

--- a/solution.py
+++ b/solution.py
@@ -10,6 +10,12 @@
 BLOCK = 128
 Q_DEV = 16
 NEG = -1e30
+lift_the_seats_all = lambda arr, shard_axis: jnp.concatenate(
+    jax.lax.all_to_all(
+        jnp.stack(jnp.split(arr, jax.lax.axis_size(shard_axis), axis=1), axis=0), shard_axis, 0, 0
+    ),
+    axis=0,
+)
 
 
 def spread_columns(table, blocks, copies, groups):
@@ -63,7 +69,7 @@
         lax.all_to_all(token_send, "seq", split_axis=1, concat_axis=0, tiled=True),
         lax.all_to_all(query_send, "seq", split_axis=1, concat_axis=0, tiled=True),
         lax.all_to_all(key_send, "seq", split_axis=1, concat_axis=0, tiled=True),
-        lax.all_to_all(value_send, "seq", split_axis=1, concat_axis=0, tiled=True),
+        lift_the_seats_all(value_send, "seq"),
     )
     query = jnp.dot(
         token_got.reshape(query_rows, D),

time: 301 us -> 319 us (1.060)
  local copies, waits for them, and re-layouts: 32 us -> 49.1 us
    all_gather x1, waiting for transfers between devices: 0.02 us -> 18.4 us  [on_device(): keys = lax.all_gather(group_keys, 'tm', axis=0, tiled=True)]
    all_gather x1, waiting for transfers between devices: 18.4 us -> 0.02 us  [on_device(): values = lax.all_gather(group_values, 'tm', axis=0, tiled=True)]
    unnamed x14 -> x29, local copies, waits for them, and re-layouts: 8.43 us -> 17.2 us
    dynamic_slice x8 -> x16, local copies, waits for them, and re-layouts: 1.12 us -> 8.91 us  [one_tile(): lax.dynamic_slice_in_dim(keys, index * key_tile, key_tile, 0)]
    dynamic_slice x16 -> x8, local copies, waits for them, and re-layouts: 9.69 us -> 7.8 us  [one_tile(): lax.dynamic_slice_in_dim(values, index * key_tile, key_tile, 0)]
  transfers between devices with their start and end apart: 6 -> 6, of which waited for: 5 -> 5; matrix products, arithmetic and copies ran while one was open for 6% -> 5% of each run, Pallas kernels for 0% -> 0%
where the time goes in v1:
time: 319 us; the launch traced here: 318 us
  waiting for transfers between devices  140 us (44%)
  blocking collectives  77.5 us (24%)
  local copies, waits for them, and re-layouts  49.1 us (15%)
  starting transfers between devices  19.5 us (6%)
  between operations  15.1 us (5%)
  matrix products  12.6 us (4%)
    all_to_all x1, blocking collectives, on_device(): lax.all_to_all(query_send, 'seq', split_axis=1, concat_axis=0, tiled=True)  65.3 us
    all_to_all x1, waiting for transfers between devices, on_device(): lax.all_to_all(token_send, 'seq', split_axis=1, concat_axis=0, tiled=True)  41.6 us
    all_gather x1, waiting for transfers between devices, on_device(): every_head = lax.all_gather(attended[None], 'seq', axis=0, tiled=True)  39 us
    all_to_all x1, waiting for transfers between devices, jax.lax.all_to_all(jnp.stack(jnp.split(arr, jax.lax.axis_size(shard_axis)...  21.6 us
    all_to_all x1, waiting for transfers between devices, on_device(): lax.all_to_all(key_send, 'seq', split_axis=1, concat_axis=0, tiled=True)  19.4 us
    all_gather x1, waiting for transfers between devices, on_device(): keys = lax.all_gather(group_keys, 'tm', axis=0, tiled=True)  18.4 us
    unnamed x29, local copies, waits for them, and re-layouts  17.2 us
    all_to_all x1, blocking collectives, on_device(): lax.all_to_all(columns, 'seq', split_axis=0, concat_axis=1, tiled=True)  12.2 us
  transfers between devices with their start and end apart: 6, of which 5 were waited for; matrix products, arithmetic and copies ran while one was open for 5% of the time, Pallas kernels for 0%

profile of v1, /device:TPU:0, one launch (start us, length us, event | category | flops | bytes accessed | tf_op | source)
XLA Modules:
  0.0 317.5 jit_solution(10437849301972547669)
XLA Ops:
  6.5 1.6 copy.104
  8.4 0.6 bitcast_dynamic-update-slice_fusion.15
  10.7 0.6 bitcast_dynamic-update-slice_fusion.14
  11.4 0.6 bitcast_dynamic-update-slice_fusion.13
  12.0 0.6 bitcast_dynamic-update-slice_fusion.12
  12.6 0.6 bitcast_dynamic-update-slice_fusion.11
  13.3 0.6 bitcast_dynamic-update-slice_fusion.10
  13.9 0.6 bitcast_dynamic-update-slice_fusion.9
  14.5 0.6 bitcast_dynamic-update-slice_fusion.8
  15.1 0.6 bitcast_dynamic-update-slice_fusion.7
  15.8 0.6 bitcast_dynamic-update-slice_fusion.6
  16.4 0.6 bitcast_dynamic-update-slice_fusion.5
  17.0 0.6 bitcast_dynamic-update-slice_fusion.4
  17.7 0.6 bitcast_dynamic-update-slice_fusion.3
  18.3 0.6 bitcast_dynamic-update-slice_fusion.2
  18.9 0.6 bitcast_dynamic-update-slice_fusion.1
  19.6 0.6 bitcast_dynamic-update-slice_fusion
  20.2 7.4 %all-to-all-start.3 = ((bf16[16,128,1,256]{3,1,2,0:T(8,128)(2,1)}), bf16[16,128,1,256]{3,1,2,0:T(8,128)(2,1)S(1)}, u32[]{:S(2)}, u32[]{:S(2)}) async-start(bf16[16,128,1,256]{3,1,2,0:T(8,128)(2,1)} %bitcast_dynamic-update-slice_fusion), calls=%async_computation.3 | async-start | bytes 2097152 | tf_op jit(solution)/shard_map/all_to_all | solution.py:14
  27.6 1.3 copy.101
  28.9 21.6 %all-to-all-done.3 = bf16[16,128,1,256]{3,1,2,0:T(8,128)(2,1)S(1)} async-done(((bf16[16,128,1,256]{3,1,2,0:T(8,128)(2,1)}), bf16[16,128,1,256]{3,1,2,0:T(8,128)(2,1)S(1)}, u32[]{:S(2)}, u32[]{:S(2)}) %all-to-all-start.3) | async-done | bytes 1048608 | tf_op jit(solution)/shard_map/all_to_all | solution.py:14
  50.5 1.0 copy-done.1
  51.5 6.8 %all-to-all-start = ((bf16[128,16,256]{0,2,1:T(8,128)(2,1)}), bf16[128,16,256]{0,2,1:T(8,128)(2,1)S(1)}, u32[]{:S(2)}, u32[]{:S(2)}) async-start(bf16[128,16,256]{0,2,1:T(8,128)(2,1)} %bitcast.3), calls=%async_computation | async-start | bytes 2097152 | tf_op jit(solution)/shard_map/all_to_all | solution.py:71
  58.3 3.5 %copy.144 = bf16[40,16,8,256]{3,2,0,1:T(8,128)(2,1)} copy(bf16[40,16,8,256]{3,2,1,0:T(8,128)(2,1)} %bitcast.117) | data formatting | bytes 5242880 | tf_op jit(solution)/shard_map/reshape;reshape | solution.py:26
  61.8 19.4 %all-to-all-done = bf16[128,16,256]{0,2,1:T(8,128)(2,1)S(1)} async-done(((bf16[128,16,256]{0,2,1:T(8,128)(2,1)}), bf16[128,16,256]{0,2,1:T(8,128)(2,1)S(1)}, u32[]{:S(2)}, u32[]{:S(2)}) %all-to-all-start) | async-done | bytes 1048608 | tf_op jit(solution)/shard_map/all_to_all | solution.py:71
  81.2 1.0 copy-done
  82.2 65.3 %all_to_all.66 = bf16[320,16,256]{2,0,1:T(8,128)(2,1)S(1)} all-to-all(bf16[320,16,256]{2,0,1:T(8,128)(2,1)} %bitcast.113), channel_id=1, replica_groups=mesh['tm'=2,'seq'=16] {'seq'}, dimensions={1} | all-to-all | bytes 5242880 | tf_op jit(solution)/shard_map/all_to_all | solution.py:70
  147.6 1.8 reshape.108
  149.4 5.2 %all-to-all-start.1 = ((bf16[16,16,5120]{2,0,1:T(8,128)(2,1)}), bf16[16,16,5120]{2,0,1:T(8,128)(2,1)}, u32[]{:S(2)}, u32[]{:S(2)}) async-start(bf16[16,16,5120]{2,0,1:T(8,128)(2,1)} %reshape.108), calls=%async_computation.1 | async-start | bytes 5242880 | tf_op jit(solution)/shard_map/all_to_all | solution.py:69
  154.7 2.3 copy.121
  157.0 2.3 copy.102
  159.4 0.6 dynamic_slice.38
  161.7 0.7 dynamic-slice_convert_fusion
  163.2 41.6 %all-to-all-done.1 = bf16[16,16,5120]{2,0,1:T(8,128)(2,1)} async-done(((bf16[16,16,5120]{2,0,1:T(8,128)(2,1)}), bf16[16,16,5120]{2,0,1:T(8,128)(2,1)}, u32[]{:S(2)}, u32[]{:S(2)}) %all-to-all-start.1) | async-done | bytes 2621472 | tf_op jit(solution)/shard_map/all_to_all | solution.py:69
  204.8 2.9 convolution_convert_fusion
  207.8 18.4 %all-gather.4.cloned.1.call-done = bf16[4096,256]{1,0:T(8,128)(2,1)} async-done(((bf16[2048,256]{1,0:T(8,128)(2,1)}), bf16[4096,256]{1,0:T(8,128)(2,1)}) %all-gather.4.cloned.1.call-update) | async-done | bytes 2097168 | tf_op jit(solution)/shard_map/all_gather | solution.py:87
  226.2 25.9 %while.20 = (s32[]{:T(128)}, f32[256,2]{0,1:T(2,128)S(1)}, f32[256,2]{0,1:T(2,128)S(1)}, f32[256,2,128]{0,2,1:T(8,128)S(1)}, f32[256,32]{0,1:T(8,128)S(1)}, /*in...) while((s32[]{:T(128)}, f32[256,2]{0,1:T(2,128)S(1)}, ...), condition=%wide.region_3.4_spmd.clone, body=%wide.region_0.3_spmd.clone.sunk | while | flops 136777248 | bytes 6461834 | solution.py:117
  226.2 1.0 constant_dynamic-slice_fusion.4
  228.0 1.0 constant_dynamic-slice_fusion.5
  229.0 0.4 fusion.56
  229.5 1.0 constant_dynamic-slice_fusion.4
  231.2 1.0 constant_dynamic-slice_fusion.5
  232.2 0.4 fusion.56
  232.7 1.0 constant_dynamic-slice_fusion.4
  234.5 1.0 constant_dynamic-slice_fusion.5
  235.5 0.4 fusion.56
  236.0 1.0 constant_dynamic-slice_fusion.4
  237.7 1.0 constant_dynamic-slice_fusion.5
  238.7 0.4 fusion.56
  239.2 1.0 constant_dynamic-slice_fusion.4
  241.0 1.0 constant_dynamic-slice_fusion.5
  242.0 0.4 fusion.56
  242.5 1.0 constant_dynamic-slice_fusion.4
  244.2 1.0 constant_dynamic-slice_fusion.5
  245.2 0.4 fusion.56
  245.7 1.0 constant_dynamic-slice_fusion.4
  247.5 1.0 constant_dynamic-slice_fusion.5
  249.0 1.0 constant_dynamic-slice_fusion.4
  250.7 1.0 constant_dynamic-slice_fusion.5
  252.2 0.8 copy.131
  252.9 2.6 copy.136
  255.5 39.0 %all-gather.8.cloned.1.call-done = bf16[16,256,256]{2,1,0:T(8,128)(2,1)} async-done(((bf16[1,256,256]{2,1,0:T(8,128)(2,1)}), bf16[16,256,256]{2,1,0:T(8,128)(2,1)}) %all-gather.8.cloned.1.call-update) | async-done | bytes 2097168 | tf_op jit(solution)/shard_map/all_gather | solution.py:124
  294.6 3.3 %fusion.17 = bf16[16,16,320]{2,1,0:T(8,128)(2,1)S(1)} fusion(bf16[16,16,16,256]{3,2,1,0:T(8,128)(2,1)} %bitcast.123, bf16[16,256,320,1]{1,0,2,3:T(8,128)(2,1)S(1)} %bitcast.119), kind=kOutput, calls=%fused_computation.25 | convolution fusion | flops 671170560 | bytes 4882432 | tf_op jit(solution)/shard_map/bcsrw,bwo->scro/dot_general | solution.py:127
  297.9 12.2 %all_to_all.67 = bf16[16,16,320]{2,1,0:T(8,128)(2,1)S(1)} all-to-all(bf16[16,16,320]{2,1,0:T(8,128)(2,1)S(1)} %fusion.17), channel_id=1, replica_groups=mesh['tm'=2,'seq'=16] {'seq'}, dimensions={0} | all-to-all | bytes 327680 | tf_op jit(solution)/shard_map/all_to_all | solution.py:131
  310.1 0.8 all_to_all.60
  (110 shorter events, 10.2 us)
Async XLA Ops:
  9.7 17.9 %copy-start.2 = (bf16[128,4096]{1,0:T(8,128)(2,1)S(1)}, bf16[128,4096]{1,0:T(8,128)(2,1)}, u32[]{:S(2)}) copy-start(bf16[128,4096]{1,0:T(8,128)(2,1)} %param.12) | copy-start | bytes 3145732
  20.2 30.3 %all-to-all-start.3 = ((bf16[16,128,1,256]{3,1,2,0:T(8,128)(2,1)}), bf16[16,128,1,256]{3,1,2,0:T(8,128)(2,1)S(1)}, u32[]{:S(2)}, u32[]{:S(2)}) async-start(bf16[16,128,1,256]{3,1,2,0:T(8,128)(2,1)} %bitcast_dynamic-update-slice_fusion), calls=%async_computation.3 | async-start | bytes 2097152 | tf_op jit(solution)/shard_map/all_to_all | solution.py:14
  50.5 1.0 copy-start.1
  51.5 29.7 %all-to-all-start = ((bf16[128,16,256]{0,2,1:T(8,128)(2,1)}), bf16[128,16,256]{0,2,1:T(8,128)(2,1)S(1)}, u32[]{:S(2)}, u32[]{:S(2)}) async-start(bf16[128,16,256]{0,2,1:T(8,128)(2,1)} %bitcast.3), calls=%async_computation | async-start | bytes 2097152 | tf_op jit(solution)/shard_map/all_to_all | solution.py:71
  81.2 1.0 copy-start
  82.2 65.3 %copy-start.3 = (bf16[16,5120]{1,0:T(8,128)(2,1)S(1)}, bf16[16,5120]{1,0:T(8,128)(2,1)}, u32[]{:S(2)}) copy-start(bf16[16,5120]{1,0:T(8,128)(2,1)} %param.9) | copy-start | bytes 491524
  149.4 55.4 %all-to-all-start.1 = ((bf16[16,16,5120]{2,0,1:T(8,128)(2,1)}), bf16[16,16,5120]{2,0,1:T(8,128)(2,1)}, u32[]{:S(2)}, u32[]{:S(2)}) async-start(bf16[16,16,5120]{2,0,1:T(8,128)(2,1)} %reshape.108), calls=%async_computation.1 | async-start | bytes 5242880 | tf_op jit(solution)/shard_map/all_to_all | solution.py:69
  154.6 53.2 %all-gather.6.cloned.1.call-start = ((), (), s32[]{:S(2)}) async-start(), calls=%async_computation.6 | async-start | bytes 3145728 | tf_op jit(solution)/shard_map/all_gather | solution.py:88
  157.0 2.4 copy-start.4
  157.0 69.2 %all-gather.4.cloned.1.call-start = ((), (), s32[]{:S(2)}) async-start(), calls=%async_computation.5 | async-start | bytes 3145728 | tf_op jit(solution)/shard_map/all_gather | solution.py:87
  159.3 135.2 %all-gather.8.cloned.1.call-start = ((), (), s32[]{:S(2)}) async-start(), calls=%async_computation.7 | async-start | bytes 2228224 | tf_op jit(solution)/shard_map/all_gather | solution.py:124
Sparse Core Ops, SparseCore 0:
  157.1 34.3 all-gather.5
  193.0 33.0 all-gather.3
  253.1 41.4 all-gather.7
